TPU v7x, 256 devices: a whole 4x4x8 slice. The times are simulated.
256 devices in a mesh: src: 32 (over z, y), tgt: 8 (over x, core).
Axes of the slice: x: 4, y: 4, z: 8, core: 2. Of those that a mesh axis runs over, the one named last changes fastest.
Arguments:
- source: bfloat16 [32768, 300], P('src'), may hold values from -70 to 70
- target: bfloat16 [16384, 300], P('tgt'), may hold values from -11 to 11
- start_map: float32 [300, 300], replicated, may hold values from -1.5 to 1.5
Outputs:
- source_soft: bfloat16 [32768, 300], P(('src', 'tgt'))
- target_soft: bfloat16 [16384, 300], P('tgt')
- polar_map: float32 [300, 300], replicated
All inputs are finite; a program needn't handle non-finite values.
Results may differ from a plain program's by a relative error of at most 0.014.
The roundings to bfloat16 on the way count: a program that leaves them out, or rounds other values in their place, can miss the bound.
Values may be sent and summed in bfloat16 or wider, within the bound.
A program may use at most 64 MiB of HBM per device.

v0:
```python
import math
import jax
import jax.numpy as jnp
from jax import lax
from jax.sharding import PartitionSpec as P

ITERS = 2
NEWTON_STEPS = 8


def polar_steps(covariance):
    highest = lax.Precision.HIGHEST
    current = covariance / jnp.sqrt(jnp.sum(covariance * covariance) + 1e-06)
    for newton in range(NEWTON_STEPS):
        gram_matrix = jnp.dot(current.T, current, precision=highest)
        current = 1.5 * current - 0.5 * jnp.dot(current, gram_matrix, precision=highest)
    return current


def merge_stats(top, total, axis):
    gathered = lax.all_gather(jnp.stack([top, total]), axis)
    tops, totals = (gathered[:, 0], gathered[:, 1])
    best = jnp.max(tops, axis=0)
    return (best, jnp.sum(totals * jnp.exp(tops - best[None]), axis=0))


def body(source, target, start_map):
    highest = lax.Precision.HIGHEST
    score_scale = 2.0 / math.sqrt(source.shape[1])
    source_f32 = source.astype(jnp.float32)
    target_f32 = target.astype(jnp.float32)
    current = start_map
    for iteration in range(ITERS):
        mapped = jnp.dot(
            source, current.astype(jnp.bfloat16), preferred_element_type=jnp.float32
        ).astype(jnp.bfloat16)
        scores = (
            lax.dot_general(
                mapped, target, (((1,), (1,)), ((), ())), preferred_element_type=jnp.float32
            )
            * score_scale
        )
        row_local = jnp.max(scores, axis=1)
        col_local = jnp.max(scores, axis=0)
        row_part = jnp.sum(jnp.exp(scores - row_local[:, None]), axis=1)
        col_part = jnp.sum(jnp.exp(scores - col_local[None, :]), axis=0)
        row_top, row_total = merge_stats(row_local, row_part, "tgt")
        col_top, col_total = merge_stats(col_local, col_part, "src")
        row_weights = (jnp.exp(scores - row_top[:, None]) / row_total[:, None]).astype(jnp.bfloat16)
        col_weights = (jnp.exp(scores - col_top[None, :]) / col_total[None, :]).astype(jnp.bfloat16)
        source_part = jnp.dot(row_weights, target, preferred_element_type=jnp.float32)
        target_part = lax.dot_general(
            col_weights, source, (((0,), (0,)), ((), ())), preferred_element_type=jnp.float32
        )
        covariance = jnp.dot(source_f32.T, source_part, precision=highest)
        covariance = covariance + jnp.dot(target_part.T, target_f32, precision=highest)
        covariance = lax.psum(covariance, ("src", "tgt"))
        if iteration == ITERS - 1:
            source_soft = lax.psum_scatter(
                source_part, "tgt", scatter_dimension=0, tiled=True
            ).astype(jnp.bfloat16)
            target_soft = lax.psum(target_part, "src").astype(jnp.bfloat16)
        current = polar_steps(covariance)
    return (source_soft, target_soft, current)


def solution(mesh):
    in_specs = (P("src", None), P("tgt", None), P())
    out_specs = (P(("src", "tgt"), None), P("tgt", None), P())
    return jax.shard_map(body, mesh=mesh, in_specs=in_specs, out_specs=out_specs, check_vma=False)
```

profile of v0, /device:TPU:8, one launch (start us, length us, event | category | flops | bytes accessed | tf_op | source)
XLA Modules:
  0.0 762.6 jit_solution(12833689186775290613)
XLA Ops:
  8.5 7.3 multiply_reduce_fusion.3
  15.8 5.1 exponential_reduce_fusion.3
  21.6 1.4 exponential_reduce_fusion.2
  23.0 52.3 %all-gather.5 = f32[32,2,2048]{2,1,0:T(2,128)S(1)} all-gather(f32[1,2,2048]{2,1,0:T(2,128)S(1)} %maximum_bitcast_fusion), channel_id=3, replica_groups=mesh['src'=32,'tgt'=8] {'src'}, dimensions={0}, use_global_device_ids=true | all-gather | bytes 540672 | tf_op jit(solution)/shard_map/all_gather | solution.py:21
  76.0 2.5 fusion
  78.5 2.2 fusion.46
  80.7 13.3 %all-gather.4 = f32[8,2,1024]{2,1,0:T(2,128)S(1)} all-gather(f32[1,2,1024]{2,1,0:T(2,128)S(1)} %maximum_bitcast_fusion.2), channel_id=2, replica_groups=mesh['src'=32,'tgt'=8] {'tgt'}, dimensions={0}, use_global_device_ids=true | all-gather | bytes 73728 | tf_op jit(solution)/shard_map/all_gather | solution.py:21
  94.1 2.5 fusion.2
  96.7 3.4 fusion.22
  100.2 249.1 %all-reduce.4.cloned.1.call-done = f32[300,300]{0,1:T(8,128)} async-done(((f32[300,300]{0,1:T(8,128)}), f32[300,300]{0,1:T(8,128)}) %all-reduce.4.cloned.1.call-update) | async-done | bytes 360016 | tf_op jit(solution)/shard_map/psum | solution.py:57
  349.3 1.7 multiply_reduce_fusion.5
  351.7 2.2 fusion.32
  353.9 2.4 fusion.21
  359.7 1.3 fusion.19
  365.6 12.7 %fusion.51 = f32[300,300]{1,0:T(8,128)S(1)} fusion(f32[300,300]{0,1:T(8,128)S(1)} %fusion.17), kind=kOutput, calls=%fused_computation.101 | convolution fusion | flops 324000000 | bytes 720000 | tf_op jit(solution)/shard_map/dot_general | solution.py:15
  384.1 5.3 multiply_reduce_fusion
  389.4 6.0 exponential_reduce_fusion
  395.4 12.9 %all-gather.6 = f32[8,2,1024]{2,1,0:T(2,128)S(1)} all-gather(f32[1,2,1024]{2,1,0:T(2,128)S(1)} %maximum_bitcast_fusion.3), channel_id=4, replica_groups=mesh['src'=32,'tgt'=8] {'tgt'}, dimensions={0}, use_global_device_ids=true | all-gather | bytes 73728 | tf_op jit(solution)/shard_map/all_gather | solution.py:21
  408.4 3.2 fusion.3
  412.8 47.7 %all-gather.7 = f32[32,2,2048]{2,1,0:T(2,128)S(1)} all-gather(f32[1,2,2048]{2,1,0:T(2,128)S(1)} %maximum_bitcast_fusion.1), channel_id=5, replica_groups=mesh['src'=32,'tgt'=8] {'src'}, dimensions={0}, use_global_device_ids=true | all-gather | bytes 540672 | tf_op jit(solution)/shard_map/all_gather | solution.py:21
  461.2 4.5 fusion.1
  465.8 1.4 copy-done.2
  467.2 2.9 convolution_add_fusion
  470.2 164.8 %all-reduce.7 = bf16[2048,300]{0,1:T(8,128)(2,1)} all-reduce(f32[2048,300]{0,1:T(8,128)} %copy-done.2), channel_id=1, replica_groups=mesh['src'=32,'tgt'=8] {'src'}, use_global_device_ids=true, to_apply=%region_19.0 | all-reduce | flops 614400 | bytes 3686400 | tf_op jit(solution)/shard_map/psum | solution.py:62
  635.0 84.4 %all-reduce.6.cloned.1.call-done = f32[300,300]{0,1:T(8,128)} async-done(((f32[300,300]{0,1:T(8,128)}), f32[300,300]{0,1:T(8,128)}) %all-reduce.6.cloned.1.call-update) | async-done | bytes 360016 | tf_op jit(solution)/shard_map/psum | solution.py:57
  719.3 1.7 multiply_reduce_fusion.4
  721.8 2.2 fusion.33
  724.0 2.4 fusion.13
  735.6 1.3 fusion.58
  739.2 1.3 fusion.7
  743.7 10.3 %reduce-scatter.2.cloned.1.call-done = f32[128,300]{0,1:T(8,128)} async-done(((f32[1024,300]{0,1:T(8,128)}), f32[128,300]{0,1:T(8,128)}) %reduce-scatter.2.cloned.1.call-update) | async-done | bytes 153616 | tf_op jit(solution)/shard_map/reduce_scatter | solution.py:59
  754.1 1.6 convert_element_type.40
  (55 shorter events, 33.1 us)
Async XLA Ops:
  7.2 1.3 copy-start
  7.2 342.1 %all-reduce.4.cloned.1.call-start = ((), (), s32[]{:S(2)}) async-start(), calls=%async_computation.1 | async-start | bytes 933888 | tf_op jit(solution)/shard_map/psum | solution.py:57
  15.8 5.8 copy-start.1
  15.8 60.2 %copy-start.4 = (bf16[1024,300]{0,1:T(8,128)(2,1)S(1)}, bf16[1024,300]{0,1:T(8,128)(2,1)}, u32[]{:S(2)}) copy-start(bf16[1024,300]{0,1:T(8,128)(2,1)} %param.3) | copy-start | bytes 1843204
  100.1 619.2 %all-reduce.6.cloned.1.call-start = ((), (), s32[]{:S(2)}) async-start(), calls=%async_computation.3 | async-start | bytes 933888 | tf_op jit(solution)/shard_map/psum | solution.py:57
  389.4 19.0 %copy-start.3 = (f32[1024,2048]{1,0:T(8,128)S(1)}, f32[1024,2048]{1,0:T(8,128)}, u32[]{:S(2)}) copy-start(f32[1024,2048]{1,0:T(8,128)} %get-tuple-element.29) | copy-start | bytes 25165828
  411.7 54.1 %copy-start.5 = (f32[1024,300]{0,1:T(8,128)}, f32[1024,300]{0,1:T(8,128)S(1)}, u32[]{:S(2)}) copy-start(f32[1024,300]{0,1:T(8,128)S(1)} %fusion.3) | copy-start | bytes 3686404
  465.8 1.4 copy-start.2
  470.1 283.9 %reduce-scatter.2.cloned.1.call-start = ((), (), s32[]{:S(2)}) async-start(), calls=%async_computation.2 | async-start | bytes 1400832 | tf_op jit(solution)/shard_map/reduce_scatter | solution.py:59
Sparse Core Ops, SparseCore 0:
  100.3 248.9 all-reduce.3
  470.3 249.0 all-reduce.5
  721.9 32.1 reduce-scatter.1
where the time goes:
time: 771 us; the launch traced here: 763 us
  waiting for transfers between devices  344 us (45%)
  blocking collectives  291 us (38%)
  matrix products  88.1 us (11%)
  other arithmetic  19.2 us (2%)
  between operations  16 us (2%)
    psum x2, waiting for transfers between devices, body(): covariance = lax.psum(covariance, ('src', 'tgt'))  333 us
    psum x1, blocking collectives, body(): target_soft = lax.psum(target_part, 'src').astype(jnp.bfloat16)  165 us
    all_gather x4, blocking collectives, merge_stats(): gathered = lax.all_gather(jnp.stack([top, total]), axis)  126 us
    dot_general x16, matrix products, polar_steps(): gram_matrix = jnp.dot(current.T, current, precision=highest)  30.9 us
    dot_general x16, matrix products, polar_steps(): jnp.dot(current, gram_matrix, precision=highest)  22.2 us
  transfers between devices with their start and end apart: 3, of which 3 were waited for; matrix products, arithmetic and copies ran while one was open for 3% of the time, Pallas kernels for 0%

commit v1 on v0

--- a/solution.py
+++ b/solution.py
@@ -6,6 +6,7 @@
 
 ITERS = 2
 NEWTON_STEPS = 8
+cover_racks_here = lambda point: lax.psum(lax.psum(point, "tgt"), axis_name="src")
 
 
 def polar_steps(covariance):
@@ -54,7 +55,7 @@
         )
         covariance = jnp.dot(source_f32.T, source_part, precision=highest)
         covariance = covariance + jnp.dot(target_part.T, target_f32, precision=highest)
-        covariance = lax.psum(covariance, ("src", "tgt"))
+        covariance = cover_racks_here(covariance)
         if iteration == ITERS - 1:
             source_soft = lax.psum_scatter(
                 source_part, "tgt", scatter_dimension=0, tiled=True

time: 771 us -> 716 us (0.929)
  waiting for transfers between devices: 344 us -> 286 us
    psum x2 -> x4, waiting for transfers between devices: 333 us -> 276 us  [the longest x2 149 us: lax.psum(lax.psum(point, 'tgt'), axis_name='src')]
  transfers between devices with their start and end apart: 3 -> 5, of which waited for: 3 -> 4; matrix products, arithmetic and copies ran while one was open for 3% -> 3% of each run, Pallas kernels for 0% -> 0%
where the time goes in v1:
time: 716 us; the launch traced here: 707 us
  blocking collectives  294 us (41%)
  waiting for transfers between devices  286 us (40%)
  matrix products  88.2 us (12%)
  other arithmetic  19.2 us (3%)
  between operations  16 us (2%)
    psum x1, blocking collectives, body(): target_soft = lax.psum(target_part, 'src').astype(jnp.bfloat16)  167 us
    psum x2, waiting for transfers between devices, lax.psum(lax.psum(point, 'tgt'), axis_name='src')  149 us
    psum x2, waiting for transfers between devices, lax.psum(point, 'tgt')  127 us
    all_gather x4, blocking collectives, merge_stats(): gathered = lax.all_gather(jnp.stack([top, total]), axis)  127 us
    dot_general x16, matrix products, polar_steps(): gram_matrix = jnp.dot(current.T, current, precision=highest)  30.9 us
    dot_general x16, matrix products, polar_steps(): jnp.dot(current, gram_matrix, precision=highest)  22.2 us
  transfers between devices with their start and end apart: 5, of which 4 were waited for; matrix products, arithmetic and copies ran while one was open for 3% of the time, Pallas kernels for 0%

profile of v1, /device:TPU:8, one launch (start us, length us, event | category | flops | bytes accessed | tf_op | source)
XLA Modules:
  0.0 707.4 jit_solution(5602931502422819669)
XLA Ops:
  8.5 7.3 %multiply_reduce_fusion.3 = (f32[1024]{0:T(1024)S(1)}, f32[1024,2048]{1,0:T(8,128)}) fusion(bf16[2048,300]{0,1:T(8,128)(2,1)S(1)} %copy-done, bf16[1024,300]{0,1:T(8,128)(2,1)} %param.3, f32[300,300]{1,0:T(8,128)} %param.5), kind=kOutput, calls=%fused_computation.11 | convolution fusion | flops 1447201664 | bytes 10595904 | tf_op jit(solution)/shard_map/dot_general | solution.py:39
  15.8 5.1 exponential_reduce_fusion.3
  21.6 1.4 exponential_reduce_fusion.2
  23.0 52.3 %all-gather.5 = f32[32,2,2048]{2,1,0:T(2,128)S(1)} all-gather(f32[1,2,2048]{2,1,0:T(2,128)S(1)} %maximum_bitcast_fusion), channel_id=3, replica_groups=mesh['src'=32,'tgt'=8] {'src'}, dimensions={0}, use_global_device_ids=true | all-gather | bytes 540672 | tf_op jit(solution)/shard_map/all_gather | solution.py:22
  76.0 2.5 fusion
  78.5 2.2 fusion.46
  80.7 13.3 %all-gather.4 = f32[8,2,1024]{2,1,0:T(2,128)S(1)} all-gather(f32[1,2,1024]{2,1,0:T(2,128)S(1)} %maximum_bitcast_fusion.2), channel_id=2, replica_groups=mesh['src'=32,'tgt'=8] {'tgt'}, dimensions={0}, use_global_device_ids=true | all-gather | bytes 73728 | tf_op jit(solution)/shard_map/all_gather | solution.py:22
  94.1 2.5 fusion.2
  96.7 3.4 fusion.22
  100.2 63.2 %all-reduce.6.cloned.1.call-done = f32[300,300]{0,1:T(8,128)} async-done(((f32[300,300]{0,1:T(8,128)}), f32[300,300]{0,1:T(8,128)}) %all-reduce.6.cloned.1.call-update) | async-done | bytes 360016 | tf_op jit(solution)/shard_map/psum | solution.py:9
  163.5 148.7 %all-reduce.8.cloned.1.call-done = f32[300,300]{0,1:T(8,128)} async-done(((f32[300,300]{0,1:T(8,128)}), f32[300,300]{0,1:T(8,128)}) %all-reduce.8.cloned.1.call-update) | async-done | bytes 360016 | tf_op jit(solution)/shard_map/psum | solution.py:9
  312.1 1.7 multiply_reduce_fusion.5
  314.6 2.2 fusion.32
  316.8 2.4 fusion.21
  322.6 1.3 fusion.19
  328.4 12.7 %fusion.51 = f32[300,300]{1,0:T(8,128)S(1)} fusion(f32[300,300]{0,1:T(8,128)S(1)} %fusion.17), kind=kOutput, calls=%fused_computation.101 | convolution fusion | flops 324000000 | bytes 720000 | tf_op jit(solution)/shard_map/dot_general | solution.py:16
  347.0 5.3 multiply_reduce_fusion
  352.3 6.0 exponential_reduce_fusion
  358.3 13.1 %all-gather.6 = f32[8,2,1024]{2,1,0:T(2,128)S(1)} all-gather(f32[1,2,1024]{2,1,0:T(2,128)S(1)} %maximum_bitcast_fusion.3), channel_id=4, replica_groups=mesh['src'=32,'tgt'=8] {'tgt'}, dimensions={0}, use_global_device_ids=true | all-gather | bytes 73728 | tf_op jit(solution)/shard_map/all_gather | solution.py:22
  371.5 3.2 fusion.3
  375.9 48.1 %all-gather.7 = f32[32,2,2048]{2,1,0:T(2,128)S(1)} all-gather(f32[1,2,2048]{2,1,0:T(2,128)S(1)} %maximum_bitcast_fusion.1), channel_id=5, replica_groups=mesh['src'=32,'tgt'=8] {'src'}, dimensions={0}, use_global_device_ids=true | all-gather | bytes 540672 | tf_op jit(solution)/shard_map/all_gather | solution.py:22
  424.7 4.5 fusion.1
  429.3 1.4 copy-done.2
  430.7 2.9 convolution_add_fusion
  433.7 63.9 %all-reduce.10.cloned.1.call-done = f32[300,300]{0,1:T(8,128)} async-done(((f32[300,300]{0,1:T(8,128)}), f32[300,300]{0,1:T(8,128)}) %all-reduce.10.cloned.1.call-update) | async-done | bytes 360016 | tf_op jit(solution)/shard_map/psum | solution.py:9
  497.6 166.7 %all-reduce.13 = bf16[2048,300]{0,1:T(8,128)(2,1)} all-reduce(f32[2048,300]{0,1:T(8,128)} %copy-done.2), channel_id=1, replica_groups=mesh['src'=32,'tgt'=8] {'src'}, use_global_device_ids=true, to_apply=%region_20.0 | all-reduce | flops 614400 | bytes 3686400 | tf_op jit(solution)/shard_map/psum | solution.py:63
  664.4 1.7 multiply_reduce_fusion.4
  666.9 2.2 fusion.33
  669.1 2.4 fusion.13
  680.7 1.3 fusion.58
  688.8 10.1 %reduce-scatter.2.cloned.1.call-done = f32[128,300]{0,1:T(8,128)} async-done(((f32[1024,300]{0,1:T(8,128)}), f32[128,300]{0,1:T(8,128)}) %reduce-scatter.2.cloned.1.call-update) | async-done | bytes 153616 | tf_op jit(solution)/shard_map/reduce_scatter | solution.py:60
  698.9 1.6 convert_element_type.40
  (61 shorter events, 34.5 us)
Async XLA Ops:
  7.2 1.3 copy-start
  7.2 156.2 %all-reduce.6.cloned.1.call-start = ((), (), s32[]{:S(2)}) async-start(), calls=%async_computation.1 | async-start | bytes 933888 | tf_op jit(solution)/shard_map/psum | solution.py:9
  15.8 5.8 copy-start.1
  15.8 60.2 %copy-start.4 = (bf16[1024,300]{0,1:T(8,128)(2,1)S(1)}, bf16[1024,300]{0,1:T(8,128)(2,1)}, u32[]{:S(2)}) copy-start(bf16[1024,300]{0,1:T(8,128)(2,1)} %param.3) | copy-start | bytes 1843204
  100.1 212.0 %all-reduce.8.cloned.1.call-start = ((), (), s32[]{:S(2)}) async-start(), calls=%async_computation.2 | async-start | bytes 933888 | tf_op jit(solution)/shard_map/psum | solution.py:9
  163.4 334.2 %all-reduce.10.cloned.1.call-start = ((), (), s32[]{:S(2)}) async-start(), calls=%async_computation.4 | async-start | bytes 933888 | tf_op jit(solution)/shard_map/psum | solution.py:9
  352.3 19.2 %copy-start.3 = (f32[1024,2048]{1,0:T(8,128)S(1)}, f32[1024,2048]{1,0:T(8,128)}, u32[]{:S(2)}) copy-start(f32[1024,2048]{1,0:T(8,128)} %get-tuple-element.29) | copy-start | bytes 25165828
  374.7 54.5 %copy-start.5 = (f32[1024,300]{0,1:T(8,128)}, f32[1024,300]{0,1:T(8,128)S(1)}, u32[]{:S(2)}) copy-start(f32[1024,300]{0,1:T(8,128)S(1)} %fusion.3) | copy-start | bytes 3686404
  429.2 1.4 copy-start.2
  433.6 230.8 %all-reduce.12.cloned.1.call-start = ((), (), s32[]{:S(2)}) async-start(), calls=%async_computation.5 | async-start | bytes 933888 | tf_op jit(solution)/shard_map/psum | solution.py:9
  497.6 201.3 %reduce-scatter.2.cloned.1.call-start = ((), (), s32[]{:S(2)}) async-start(), calls=%async_computation.3 | async-start | bytes 1400832 | tf_op jit(solution)/shard_map/reduce_scatter | solution.py:60
Sparse Core Ops, SparseCore 0:
  100.3 63.0 all-reduce.5
  167.2 144.9 all-reduce.7
  433.7 63.7 all-reduce.9
  501.2 145.0 all-reduce.11
  664.5 34.3 reduce-scatter.1
